TPU v7x, 32 devices: a whole 2x2x4 slice. The times are simulated.
32 devices in a mesh: snap: 8 (over z, x), feat: 4 (over y, core).
Axes of the slice: x: 2, y: 2, z: 4, core: 2. Of those that a mesh axis runs over, the one named last changes fastest.
Arguments:
- node_features: bfloat16 [16, 512, 256], P('snap', None, 'feat'), may hold values from -6 to 6
- tile_rows: int32 [16, 8], P('snap'), may hold values from 0 to 3
- tile_cols: int32 [16, 8], P('snap'), may hold values from 0 to 3, as said below
- tile_counts: int32 [16], P('snap'), may hold values from 4 to 8, as said below
- tile_values: bfloat16 [16, 8, 128, 128], P('snap'), may hold values from -0.5 to 0.5
- layer_one: bfloat16 [256, 256], replicated, may hold values from -0.375 to 0.375
- layer_two: bfloat16 [256, 256], replicated, may hold values from -0.375 to 0.375
- query_weight: bfloat16 [256, 256], replicated, may hold values from -1.25 to 1.25
- key_weight: bfloat16 [256, 256], replicated, may hold values from -1.25 to 1.25
- value_weight: bfloat16 [256, 256], replicated, may hold values from -0.375 to 0.375
- out_weight: bfloat16 [256, 256], replicated, may hold values from -0.375 to 0.375
Outputs:
- evolved: bfloat16 [16, 512, 256], P('snap', None, 'feat')
Inputs may be any that keep to these rules, and one draw needn't show every extreme that they name: `tile_cols`: block columns of the tile slots; a coordinate pair may be listed more than once, and such tiles add. `tile_counts`: some snapshot uses all 8 slots.
All inputs are finite; a program needn't handle non-finite values.
Results may differ from a plain program's by a relative error of at most 0.02.
The roundings to bfloat16 on the way count: a program that leaves them out, or rounds other values in their place, can miss the bound.
Values may be sent and summed in bfloat16 or wider, within the bound.
A program may use at most 64 MiB of HBM per device.

v0:
```python
import jax
import jax.numpy as jnp
from jax import lax
from jax.sharding import PartitionSpec as P

HEADS = 8
masked_score = -1e30


def spread_padded(features, tile_block, block_rows, block_cols, slot_count):
    vert_count, feat_width = features.shape
    tile_side = tile_block.shape[1]
    slot_total = tile_block.shape[0]
    block_count = vert_count // tile_side
    blocked = features.reshape(block_count, tile_side, feat_width)
    picked_blocks = blocked[block_cols]
    live_slots = jnp.arange(slot_total, dtype=jnp.int32) < slot_count
    products = jnp.einsum(
        "irc,icf->irf", tile_block, picked_blocks, preferred_element_type=jnp.float32
    )
    products = products * live_slots.astype(jnp.float32)[:, None, None]
    membership = (
        (block_rows[None, :] == jnp.arange(block_count, dtype=jnp.int32)[:, None])
        & live_slots[None, :]
    ).astype(jnp.float32)
    summed = jnp.dot(
        membership,
        products.reshape(slot_total, tile_side * feat_width),
        precision=lax.Precision.HIGHEST,
    )
    return summed.reshape(vert_count, feat_width).astype(jnp.bfloat16)


def attend_local(hidden, query_weight, key_weight, value_weight, out_weight):
    snaps, verts, model_width = hidden.shape
    head_dim = model_width // HEADS
    flat = hidden.reshape(snaps * verts, model_width)

    def project(weight):
        return (
            jnp.dot(flat, weight, preferred_element_type=jnp.float32)
            .astype(jnp.bfloat16)
            .reshape(snaps, verts, HEADS, head_dim)
        )

    query_heads = project(query_weight)
    key_heads = project(key_weight)
    value_heads = project(value_weight)
    scores = jnp.einsum(
        "tvhd,uvhd->vhtu", query_heads, key_heads, preferred_element_type=jnp.float32
    ) * head_dim ** (-0.5)
    causal = (
        jnp.arange(snaps, dtype=jnp.int32)[:, None] >= jnp.arange(snaps, dtype=jnp.int32)[None, :]
    )
    scores = jnp.where(causal, scores, masked_score)
    row_max = jnp.max(scores, axis=-1, keepdims=True)
    lifted = jnp.exp(scores - row_max)
    weights = (lifted / jnp.sum(lifted, axis=-1, keepdims=True)).astype(jnp.bfloat16)
    context = jnp.einsum(
        "vhtu,uvhd->tvhd", weights, value_heads, preferred_element_type=jnp.float32
    ).astype(jnp.bfloat16)
    context = context.reshape(snaps * verts, model_width)
    result = flat.astype(jnp.float32) + jnp.dot(
        context, out_weight, preferred_element_type=jnp.float32
    )
    return result.astype(jnp.bfloat16).reshape(snaps, verts, model_width)


def on_device(
    node_features,
    tile_rows,
    tile_cols,
    tile_counts,
    tile_values,
    layer_one,
    layer_two,
    query_weight,
    key_weight,
    value_weight,
    out_weight,
):
    snap_dev, vert_count, feat_width = node_features.shape
    feat_index = lax.axis_index("feat")

    def spread_all(features):
        spread_pieces = []
        for snapshot in range(snap_dev):
            spread_pieces.append(
                spread_padded(
                    features[snapshot],
                    tile_values[snapshot],
                    tile_rows[snapshot],
                    tile_cols[snapshot],
                    tile_counts[snapshot],
                )
            )
        return jnp.stack(spread_pieces, axis=0)

    def convolve(features, weight):
        spread_rows = spread_all(features).reshape(snap_dev * vert_count, feat_width)
        own_columns = lax.dynamic_slice_in_dim(weight, feat_index * feat_width, feat_width, 1)
        mixed_sum = jnp.dot(
            lax.all_gather(spread_rows, "feat", axis=1, tiled=True),
            own_columns,
            preferred_element_type=jnp.float32,
        )
        mixed_sum = mixed_sum.reshape(snap_dev, vert_count, feat_width)
        return (features.astype(jnp.float32) + jnp.maximum(mixed_sum, 0.0)).astype(jnp.bfloat16)

    hidden_one = convolve(node_features, layer_one)
    hidden_two = convolve(hidden_one, layer_two)
    vertex_rows = lax.all_to_all(
        lax.all_to_all(hidden_two, "snap", split_axis=1, concat_axis=0, tiled=True),
        "feat",
        split_axis=1,
        concat_axis=2,
        tiled=True,
    )
    attended = attend_local(vertex_rows, query_weight, key_weight, value_weight, out_weight)
    return lax.all_to_all(
        lax.all_to_all(attended, "feat", split_axis=2, concat_axis=1, tiled=True),
        "snap",
        split_axis=0,
        concat_axis=1,
        tiled=True,
    )


def solution(mesh):
    placed = (
        P("snap", None, "feat"),
        P("snap", None),
        P("snap", None),
        P("snap"),
        P("snap", None, None, None),
        P(),
        P(),
        P(),
        P(),
        P(),
        P(),
    )
    return jax.shard_map(
        on_device, mesh=mesh, in_specs=placed, out_specs=P("snap", None, "feat"), check_vma=False
    )
```

profile of v0, /device:TPU:0, one launch (start us, length us, event | category | flops | bytes accessed | tf_op | source)
XLA Modules:
  0.0 81.3 jit_solution(12368943352257759503)
XLA Ops:
  0.0 0.7 copy-done.9
  0.7 0.9 %fusion.47 = (bf16[1,512,64]{1,2,0:T(8,128)(2,1)S(1)}, bf16[1,512,64]{1,2,0:T(8,128)(2,1)S(1)}) fusion(bf16[2,512,64]{1,2,0:T(8,128)(2,1)} %param.11), kind=kLoop, calls=%fused_computation.79 | loop fusion | bytes 262144 | tf_op jit(solution)/shard_map/slice | solution.py:90
  1.7 0.6 copy-done.8
  2.4 0.6 fusion.48
  3.0 0.6 iota_compare_fusion.4
  3.6 0.6 gather_fusion
  4.2 0.3 fusion.8
  4.5 0.2 copy.104
  4.7 0.2 reshape.167
  4.9 0.5 copy-done.10
  5.4 0.2 convolution_convert_fusion.3
  5.9 0.6 iota_compare_fusion.3
  6.5 0.6 gather_fusion.1
  7.1 0.3 fusion.7
  7.4 0.2 copy.106
  7.6 0.2 reshape.168
  7.8 0.2 convolution_convert_fusion.2
  8.4 8.7 %all_gather.6 = bf16[1024,256]{0,1:T(8,128)(2,1)S(1)} all-gather(bf16[1024,64]{0,1:T(8,128)(2,1)S(1)} %copy.107), channel_id=1, replica_groups=mesh['snap'=8,'feat'=4] {'feat'}, dimensions={1}, use_global_device_ids=true | all-gather | bytes 655360 | tf_op jit(solution)/shard_map/all_gather | solution.py:103
  17.1 0.3 convolution_maximum_fusion.1
  17.4 0.6 copy-done.2
  18.1 0.6 gather_fusion.2
  18.6 0.3 fusion.6
  18.9 0.2 copy.110
  19.1 0.2 reshape.170
  19.3 0.2 convolution_convert_fusion.1
  19.8 0.6 gather_fusion.3
  20.4 0.3 fusion.5
  20.6 0.2 copy.112
  20.9 0.2 reshape.171
  21.0 0.2 convolution_convert_fusion
  21.7 7.4 %all_gather.7 = bf16[1024,256]{0,1:T(8,128)(2,1)S(1)} all-gather(bf16[1024,64]{0,1:T(8,128)(2,1)S(1)} %copy.113), channel_id=1, replica_groups=mesh['snap'=8,'feat'=4] {'feat'}, dimensions={1}, use_global_device_ids=true | all-gather | bytes 655360 | tf_op jit(solution)/shard_map/all_gather | solution.py:103
  29.1 0.3 convolution_maximum_fusion
  29.6 0.2 reshape.211
  29.9 13.1 %all_to_all.69 = bf16[8,2,4096]{2,1,0:T(2,128)(2,1)S(1)} all-to-all(bf16[8,2,4096]{2,1,0:T(2,128)(2,1)S(1)} %reshape.211), channel_id=1, replica_groups=mesh['snap'=8,'feat'=4] {'snap'}, dimensions={0} | all-to-all | bytes 262144 | tf_op jit(solution)/shard_map/all_to_all | solution.py:113
  43.0 0.2 reshape.212
  43.4 0.9 %reshape.213 = bf16[4,2,8192]{2,1,0:T(2,128)(2,1)} reshape(bf16[64,16,64]{2,1,0:T(8,128)(2,1)S(1)} %bitcast.111) | data formatting | bytes 262144
  44.3 3.3 %all-to-all-start.1 = ((bf16[4,2,8192]{2,1,0:T(2,128)(2,1)}), bf16[4,2,8192]{2,1,0:T(2,128)(2,1)S(1)}, u32[]{:S(2)}, u32[]{:S(2)}) async-start(bf16[4,2,8192]{2,1,0:T(2,128)(2,1)} %reshape.213), calls=%async_computation.1 | async-start | bytes 262144 | tf_op jit(solution)/shard_map/all_to_all | solution.py:112
  47.7 4.6 %all-to-all-done.1 = bf16[4,2,8192]{2,1,0:T(2,128)(2,1)S(1)} async-done(((bf16[4,2,8192]{2,1,0:T(2,128)(2,1)}), bf16[4,2,8192]{2,1,0:T(2,128)(2,1)S(1)}, u32[]{:S(2)}, u32[]{:S(2)}) %all-to-all-start.1) | async-done | bytes 131104 | tf_op jit(solution)/shard_map/all_to_all | solution.py:112
  52.2 0.2 reshape.214
  52.4 0.2 copy.120
  52.7 0.2 reshape.173
  52.9 0.7 copy-done.3
  53.6 0.2 convolution_convert_fusion.6
  53.8 0.2 reshape.175
  54.0 0.7 copy-done.4
  54.7 0.2 convolution_convert_fusion.5
  54.9 0.2 reshape.176
  55.1 0.7 copy-done.5
  55.9 0.2 reshape.174
  56.2 1.0 %fusion.49 = (f32[16,8,16]{2,1,0:T(8,128)S(1)}, f32[16,8,16,16]{2,3,1,0:T(8,128)S(1)}) fusion(bf16[16,16,8,32]{3,2,1,0:T(8,128)(2,1)S(1)} %reshape.176, bf16[16,16,8,32]{3,2,1,0:T(8,128)(2,1)S(1)} %reshape.175, pred[16,16]{0,1:T(8,128)(4,1)S(1)} %iota_compare_fusion), kind=kOutput, calls=%fused_computation.81 | convolution fusion | flops 2228239 | bytes 401664 | tf_op jit(solution)/shard_map/sub | solution.py:57
  57.2 0.5 fusion.4
  57.9 0.4 reshape.177
  58.3 0.5 copy-done.6
  58.8 0.2 fusion.9
  59.0 0.9 %copy.126 = bf16[16,16,256]{1,0,2:T(8,128)(2,1)S(1)} copy(bf16[16,16,256]{2,1,0:T(8,128)(2,1)S(1)} %bitcast.115) | data formatting | bytes 262144 | tf_op jit(solution)/shard_map/reshape | solution.py:66
  60.0 1.1 %reshape.215 = bf16[4,2,8192]{2,1,0:T(2,128)(2,1)S(1)} reshape(bf16[256,16,16]{2,1,0:T(8,128)(2,1)S(1)} %bitcast.102) | data formatting | bytes 262144
  61.0 7.0 %all_to_all.70 = bf16[4,2,8192]{2,1,0:T(2,128)(2,1)S(1)} all-to-all(bf16[4,2,8192]{2,1,0:T(2,128)(2,1)S(1)} %reshape.215), channel_id=1, replica_groups=mesh['snap'=8,'feat'=4] {'feat'}, dimensions={0} | all-to-all | bytes 262144 | tf_op jit(solution)/shard_map/all_to_all | solution.py:121
  68.0 0.7 reshape.216
  68.7 1.2 %copy.134 = bf16[16,16,4,64]{3,2,1,0:T(4,128)(2,1)S(1)} copy(bf16[16,16,4,64]{1,0,3,2:T(8,128)(2,1)S(1)} %bitcast.101) | data formatting | bytes 262144 | tf_op jit(solution)/shard_map/all_to_all | solution.py:121
  69.9 0.2 reshape.217
  70.2 9.9 %all_to_all.71 = bf16[8,2,4096]{2,1,0:T(2,128)(2,1)S(1)} all-to-all(bf16[8,2,4096]{2,1,0:T(2,128)(2,1)S(1)} %reshape.217), channel_id=1, replica_groups=mesh['snap'=8,'feat'=4] {'snap'}, dimensions={0} | all-to-all | bytes 262144 | tf_op jit(solution)/shard_map/all_to_all | solution.py:120
  80.0 0.2 reshape.218
  80.3 0.2 copy.129
  80.5 0.9 %all_to_all.64 = bf16[2,512,64]{1,2,0:T(8,128)(2,1)} reshape(bf16[2,8,64,64]{2,1,3,0:T(8,128)(2,1)S(1)} %copy.129) | data formatting | bytes 262144 | tf_op jit(solution)/shard_map/all_to_all | solution.py:120
  (43 shorter events, 2.0 us)
Async XLA Ops:
  0.0 17.1 %copy-start = (bf16[256,256]{1,0:T(8,128)(2,1)S(1)}, bf16[256,256]{1,0:T(8,128)(2,1)}, u32[]{:S(2)}) copy-start(bf16[256,256]{1,0:T(8,128)(2,1)} %param.16) | copy-start | bytes 393220
  0.0 0.7 copy-start.9
  0.7 3.5 %copy-start.1 = (bf16[2,8,128,128]{3,2,1,0:T(8,128)(2,1)S(1)}, bf16[2,8,128,128]{3,2,1,0:T(8,128)(2,1)}, u32[]{:S(2)}) copy-start(bf16[2,8,128,128]{3,2,1,0:T(8,128)(2,1)} %param.15) | copy-start | bytes 1572868
  1.7 0.7 copy-start.8
  4.7 0.7 copy-start.10
  17.1 0.9 %copy-start.2 = (bf16[2,512,64]{1,2,0:T(8,128)(2,1)S(1)}, bf16[2,512,64]{1,2,0:T(8,128)(2,1)}, u32[]{:S(2)}) copy-start(bf16[2,512,64]{1,2,0:T(8,128)(2,1)} %param.11) | copy-start | bytes 393220
  21.7 7.4 %copy-start.7 = (bf16[256,256]{1,0:T(8,128)(2,1)S(1)}, bf16[256,256]{1,0:T(8,128)(2,1)}, u32[]{:S(2)}) copy-start(bf16[256,256]{1,0:T(8,128)(2,1)} %param.17) | copy-start | bytes 393220
  44.3 7.9 %all-to-all-start.1 = ((bf16[4,2,8192]{2,1,0:T(2,128)(2,1)}), bf16[4,2,8192]{2,1,0:T(2,128)(2,1)S(1)}, u32[]{:S(2)}, u32[]{:S(2)}) async-start(bf16[4,2,8192]{2,1,0:T(2,128)(2,1)} %reshape.213), calls=%async_computation.1 | async-start | bytes 262144 | tf_op jit(solution)/shard_map/all_to_all | solution.py:112
  52.7 0.9 %copy-start.3 = (bf16[256,256]{1,0:T(8,128)(2,1)S(1)}, bf16[256,256]{1,0:T(8,128)(2,1)}, u32[]{:S(2)}) copy-start(bf16[256,256]{1,0:T(8,128)(2,1)} %param.18) | copy-start | bytes 393220
  53.8 0.9 %copy-start.4 = (bf16[256,256]{1,0:T(8,128)(2,1)S(1)}, bf16[256,256]{1,0:T(8,128)(2,1)}, u32[]{:S(2)}) copy-start(bf16[256,256]{1,0:T(8,128)(2,1)} %param.19) | copy-start | bytes 393220
  54.9 0.9 %copy-start.5 = (bf16[256,256]{1,0:T(8,128)(2,1)S(1)}, bf16[256,256]{1,0:T(8,128)(2,1)}, u32[]{:S(2)}) copy-start(bf16[256,256]{1,0:T(8,128)(2,1)} %param.20) | copy-start | bytes 393220
  57.9 0.9 %copy-start.6 = (bf16[256,256]{1,0:T(8,128)(2,1)S(1)}, bf16[256,256]{1,0:T(8,128)(2,1)}, u32[]{:S(2)}) copy-start(bf16[256,256]{1,0:T(8,128)(2,1)} %param.21) | copy-start | bytes 393220
where the time goes:
time: 81.8 us; the launch traced here: 81.3 us
  blocking collectives  46 us (56%)
  local copies, waits for them, and re-layouts  20.4 us (25%)
  matrix products  4.96 us (6%)
  waiting for transfers between devices  4.55 us (6%)
  starting transfers between devices  3.33 us (4%)
  other arithmetic  1.48 us (2%)
    all_gather x2, blocking collectives, convolve(): lax.all_gather(spread_rows, 'feat', axis=1, tiled=True)  16.1 us
    all_to_all x1, blocking collectives, on_device(): lax.all_to_all(hidden_two, 'snap', split_axis=1, concat_axis=0, tiled=True)  13.1 us
    all_to_all x1, blocking collectives, on_device(): lax.all_to_all(lax.all_to_all(attended, 'feat', split_axis=2, concat_axis...  9.86 us
    unnamed x30, local copies, waits for them, and re-layouts  8.75 us
    all_to_all x1, blocking collectives, on_device(): lax.all_to_all(attended, 'feat', split_axis=2, concat_axis=1, tiled=True)  6.99 us
    all_to_all x1, waiting for transfers between devices, on_device(): lax.all_to_all(lax.all_to_all(hidden_two, 'snap', split_axis=1, concat_ax...  4.55 us
    all_to_all x1, starting transfers between devices, on_device(): lax.all_to_all(lax.all_to_all(hidden_two, 'snap', split_axis=1, concat_ax...  3.33 us
    gather x4, local copies, waits for them, and re-layouts, spread_padded(): picked_blocks = blocked[block_cols]  2.29 us
  transfers between devices with their start and end apart: 1, of which 1 were waited for; matrix products, arithmetic and copies ran while one was open for 0% of the time, Pallas kernels for 0%

commit v1 on v0

--- a/solution.py
+++ b/solution.py
@@ -5,6 +5,11 @@
 
 HEADS = 8
 masked_score = -1e30
+
+
+def gathered_along(x, axis, dim):
+    blocks = lax.all_gather(x, axis)
+    return jnp.concatenate(blocks, axis=dim)
 
 
 def spread_padded(features, tile_block, block_rows, block_cols, slot_count):
@@ -100,9 +105,7 @@
         spread_rows = spread_all(features).reshape(snap_dev * vert_count, feat_width)
         own_columns = lax.dynamic_slice_in_dim(weight, feat_index * feat_width, feat_width, 1)
         mixed_sum = jnp.dot(
-            lax.all_gather(spread_rows, "feat", axis=1, tiled=True),
-            own_columns,
-            preferred_element_type=jnp.float32,
+            gathered_along(spread_rows, "feat", 1), own_columns, preferred_element_type=jnp.float32
         )
         mixed_sum = mixed_sum.reshape(snap_dev, vert_count, feat_width)
         return (features.astype(jnp.float32) + jnp.maximum(mixed_sum, 0.0)).astype(jnp.bfloat16)

time: 81.8 us -> 82.9 us (1.013)
  local copies, waits for them, and re-layouts: 20.4 us -> 21.6 us
where the time goes in v1:
time: 82.9 us; the launch traced here: 82.3 us
  blocking collectives  45.9 us (55%)
  local copies, waits for them, and re-layouts  21.6 us (26%)
  matrix products  4.97 us (6%)
  waiting for transfers between devices  4.37 us (5%)
  starting transfers between devices  3.51 us (4%)
  other arithmetic  1.42 us (2%)
    all_gather x2, blocking collectives, gathered_along(): blocks = lax.all_gather(x, axis)  16 us
    all_to_all x1, blocking collectives, on_device(): lax.all_to_all(hidden_two, 'snap', split_axis=1, concat_axis=0, tiled=True)  13.1 us
    all_to_all x1, blocking collectives, on_device(): lax.all_to_all(lax.all_to_all(attended, 'feat', split_axis=2, concat_axis...  9.85 us
    unnamed x30, local copies, waits for them, and re-layouts  9.2 us
    all_to_all x1, blocking collectives, on_device(): lax.all_to_all(attended, 'feat', split_axis=2, concat_axis=1, tiled=True)  6.99 us
    all_to_all x1, waiting for transfers between devices, on_device(): lax.all_to_all(lax.all_to_all(hidden_two, 'snap', split_axis=1, concat_ax...  4.37 us
    all_to_all x1, starting transfers between devices, on_device(): lax.all_to_all(lax.all_to_all(hidden_two, 'snap', split_axis=1, concat_ax...  3.51 us
    gather x4, local copies, waits for them, and re-layouts, spread_padded(): picked_blocks = blocked[block_cols]  2.29 us
  transfers between devices with their start and end apart: 1, of which 1 were waited for; matrix products, arithmetic and copies ran while one was open for 0% of the time, Pallas kernels for 0%

profile of v1, /device:TPU:0, one launch (start us, length us, event | category | flops | bytes accessed | tf_op | source)
XLA Modules:
  0.0 82.3 jit_solution(11732548535319540781)
XLA Ops:
  0.0 0.7 copy-done.8
  0.7 0.9 %fusion.53 = (bf16[1,512,64]{1,2,0:T(8,128)(2,1)S(1)}, bf16[1,512,64]{1,2,0:T(8,128)(2,1)S(1)}) fusion(bf16[2,512,64]{1,2,0:T(8,128)(2,1)} %param.11), kind=kLoop, calls=%fused_computation.83 | loop fusion | bytes 262144 | tf_op jit(solution)/shard_map/slice | solution.py:95
  1.7 0.6 copy-done.7
  2.4 0.6 fusion.54
  3.0 0.6 iota_compare_fusion.4
  3.6 0.6 gather_fusion
  4.2 0.3 fusion.10
  4.5 0.2 copy.90
  4.7 0.2 reshape.169
  4.9 0.5 copy-done.9
  5.4 0.2 convolution_convert_fusion.3
  5.9 0.6 iota_compare_fusion.3
  6.5 0.6 gather_fusion.1
  7.1 0.3 fusion.9
  7.4 0.2 copy.92
  7.6 0.2 reshape.170
  7.8 0.2 convolution_convert_fusion.2
  8.4 8.7 %all_gather.6 = bf16[4,1024,64]{1,2,0:T(8,128)(2,1)S(1)} all-gather(bf16[1,1024,64]{1,2,0:T(8,128)(2,1)S(1)} %copy.93), channel_id=1, replica_groups=mesh['snap'=8,'feat'=4] {'feat'}, dimensions={0}, use_global_device_ids=true | all-gather | bytes 655360 | tf_op jit(solution)/shard_map/all_gather | solution.py:11
  17.1 0.4 dot_general.56
  17.5 0.5 copy-done.5
  18.0 0.3 fusion.11
  18.4 0.6 gather_fusion.2
  18.9 0.3 fusion.7
  19.2 0.2 copy.97
  19.4 0.2 reshape.172
  19.6 0.2 convolution_convert_fusion.1
  20.1 0.6 gather_fusion.3
  20.7 0.3 fusion.6
  20.9 0.2 copy.99
  21.2 0.2 reshape.173
  21.3 0.2 convolution_convert_fusion
  22.0 7.3 %all_gather.7 = bf16[4,1024,64]{1,2,0:T(8,128)(2,1)S(1)} all-gather(bf16[1,1024,64]{1,2,0:T(8,128)(2,1)S(1)} %copy.100), channel_id=1, replica_groups=mesh['snap'=8,'feat'=4] {'feat'}, dimensions={0}, use_global_device_ids=true | all-gather | bytes 655360 | tf_op jit(solution)/shard_map/all_gather | solution.py:11
  29.2 0.4 dot_general.62
  29.6 0.5 copy-done.10
  30.1 0.3 fusion.12
  30.6 0.2 reshape.215
  30.9 13.1 %all_to_all.69 = bf16[8,2,4096]{2,1,0:T(2,128)(2,1)S(1)} all-to-all(bf16[8,2,4096]{2,1,0:T(2,128)(2,1)S(1)} %reshape.215), channel_id=1, replica_groups=mesh['snap'=8,'feat'=4] {'snap'}, dimensions={0} | all-to-all | bytes 262144 | tf_op jit(solution)/shard_map/all_to_all | solution.py:116
  44.0 0.2 reshape.216
  44.4 0.9 %reshape.217 = bf16[4,2,8192]{2,1,0:T(2,128)(2,1)} reshape(bf16[64,16,64]{2,1,0:T(8,128)(2,1)S(1)} %bitcast.113) | data formatting | bytes 262144
  45.3 3.5 %all-to-all-start.1 = ((bf16[4,2,8192]{2,1,0:T(2,128)(2,1)}), bf16[4,2,8192]{2,1,0:T(2,128)(2,1)S(1)}, u32[]{:S(2)}, u32[]{:S(2)}) async-start(bf16[4,2,8192]{2,1,0:T(2,128)(2,1)} %reshape.217), calls=%async_computation.1 | async-start | bytes 262144 | tf_op jit(solution)/shard_map/all_to_all | solution.py:115
  48.9 4.4 %all-to-all-done.1 = bf16[4,2,8192]{2,1,0:T(2,128)(2,1)S(1)} async-done(((bf16[4,2,8192]{2,1,0:T(2,128)(2,1)}), bf16[4,2,8192]{2,1,0:T(2,128)(2,1)S(1)}, u32[]{:S(2)}, u32[]{:S(2)}) %all-to-all-start.1) | async-done | bytes 131104 | tf_op jit(solution)/shard_map/all_to_all | solution.py:115
  53.2 0.2 reshape.218
  53.5 0.2 copy.108
  53.7 0.2 reshape.175
  53.9 0.7 copy-done.2
  54.8 0.2 reshape.177
  55.0 0.7 copy-done.3
  55.9 0.2 reshape.178
  56.1 0.7 copy-done.4
  57.0 0.2 reshape.176
  57.2 1.0 %fusion.55 = (f32[16,8,16]{2,1,0:T(8,128)S(1)}, f32[16,8,16,16]{2,3,1,0:T(8,128)S(1)}) fusion(bf16[16,16,8,32]{3,2,1,0:T(8,128)(2,1)S(1)} %reshape.178, bf16[16,16,8,32]{3,2,1,0:T(8,128)(2,1)S(1)} %reshape.177, pred[16,16]{0,1:T(8,128)(4,1)S(1)} %iota_compare_fusion), kind=kOutput, calls=%fused_computation.85 | convolution fusion | flops 2228239 | bytes 401664 | tf_op jit(solution)/shard_map/sub | solution.py:62
  58.3 0.5 fusion.4
  58.9 0.4 reshape.179
  59.3 0.5 copy-done.6
  60.0 0.9 %copy.114 = bf16[16,16,256]{1,0,2:T(8,128)(2,1)S(1)} copy(bf16[16,16,256]{2,1,0:T(8,128)(2,1)S(1)} %bitcast.117) | data formatting | bytes 262144 | tf_op jit(solution)/shard_map/reshape | solution.py:71
  61.0 1.1 %reshape.219 = bf16[4,2,8192]{2,1,0:T(2,128)(2,1)S(1)} reshape(bf16[256,16,16]{2,1,0:T(8,128)(2,1)S(1)} %bitcast.104) | data formatting | bytes 262144
  62.0 7.0 %all_to_all.70 = bf16[4,2,8192]{2,1,0:T(2,128)(2,1)S(1)} all-to-all(bf16[4,2,8192]{2,1,0:T(2,128)(2,1)S(1)} %reshape.219), channel_id=1, replica_groups=mesh['snap'=8,'feat'=4] {'feat'}, dimensions={0} | all-to-all | bytes 262144 | tf_op jit(solution)/shard_map/all_to_all | solution.py:124
  69.0 0.7 reshape.220
  69.7 1.2 %copy.122 = bf16[16,16,4,64]{3,2,1,0:T(4,128)(2,1)S(1)} copy(bf16[16,16,4,64]{1,0,3,2:T(8,128)(2,1)S(1)} %bitcast.103) | data formatting | bytes 262144 | tf_op jit(solution)/shard_map/all_to_all | solution.py:124
  71.0 0.2 reshape.221
  71.2 9.9 %all_to_all.71 = bf16[8,2,4096]{2,1,0:T(2,128)(2,1)S(1)} all-to-all(bf16[8,2,4096]{2,1,0:T(2,128)(2,1)S(1)} %reshape.221), channel_id=1, replica_groups=mesh['snap'=8,'feat'=4] {'snap'}, dimensions={0} | all-to-all | bytes 262144 | tf_op jit(solution)/shard_map/all_to_all | solution.py:123
  81.1 0.2 reshape.222
  81.3 0.2 copy.117
  81.5 0.9 %all_to_all.64 = bf16[2,512,64]{1,2,0:T(8,128)(2,1)} reshape(bf16[2,8,64,64]{2,1,3,0:T(8,128)(2,1)S(1)} %copy.117) | data formatting | bytes 262144 | tf_op jit(solution)/shard_map/all_to_all | solution.py:123
  (43 shorter events, 2.5 us)
Async XLA Ops:
  0.0 17.4 %copy-start = (bf16[256,256]{1,0:T(8,128)(2,1)S(1)}, bf16[256,256]{1,0:T(8,128)(2,1)}, u32[]{:S(2)}) copy-start(bf16[256,256]{1,0:T(8,128)(2,1)} %param.16) | copy-start | bytes 393220
  0.0 0.7 copy-start.8
  0.7 3.5 %copy-start.1 = (bf16[2,8,128,128]{3,2,1,0:T(8,128)(2,1)S(1)}, bf16[2,8,128,128]{3,2,1,0:T(8,128)(2,1)}, u32[]{:S(2)}) copy-start(bf16[2,8,128,128]{3,2,1,0:T(8,128)(2,1)} %param.15) | copy-start | bytes 1572868
  1.7 0.7 copy-start.7
  4.7 0.7 copy-start.9
  17.1 0.9 %copy-start.5 = (bf16[2,512,64]{1,2,0:T(8,128)(2,1)S(1)}, bf16[2,512,64]{1,2,0:T(8,128)(2,1)}, u32[]{:S(2)}) copy-start(bf16[2,512,64]{1,2,0:T(8,128)(2,1)} %param.11) | copy-start | bytes 393220
  29.2 0.9 %copy-start.10 = (bf16[256,256]{1,0:T(8,128)(2,1)S(1)}, bf16[256,256]{1,0:T(8,128)(2,1)}, u32[]{:S(2)}) copy-start(bf16[256,256]{1,0:T(8,128)(2,1)} %param.17) | copy-start | bytes 393220
  45.3 7.9 %all-to-all-start.1 = ((bf16[4,2,8192]{2,1,0:T(2,128)(2,1)}), bf16[4,2,8192]{2,1,0:T(2,128)(2,1)S(1)}, u32[]{:S(2)}, u32[]{:S(2)}) async-start(bf16[4,2,8192]{2,1,0:T(2,128)(2,1)} %reshape.217), calls=%async_computation.1 | async-start | bytes 262144 | tf_op jit(solution)/shard_map/all_to_all | solution.py:115
  53.7 0.9 %copy-start.2 = (bf16[256,256]{1,0:T(8,128)(2,1)S(1)}, bf16[256,256]{1,0:T(8,128)(2,1)}, u32[]{:S(2)}) copy-start(bf16[256,256]{1,0:T(8,128)(2,1)} %param.18) | copy-start | bytes 393220
  54.8 0.9 %copy-start.3 = (bf16[256,256]{1,0:T(8,128)(2,1)S(1)}, bf16[256,256]{1,0:T(8,128)(2,1)}, u32[]{:S(2)}) copy-start(bf16[256,256]{1,0:T(8,128)(2,1)} %param.19) | copy-start | bytes 393220
  55.9 0.9 %copy-start.4 = (bf16[256,256]{1,0:T(8,128)(2,1)S(1)}, bf16[256,256]{1,0:T(8,128)(2,1)}, u32[]{:S(2)}) copy-start(bf16[256,256]{1,0:T(8,128)(2,1)} %param.20) | copy-start | bytes 393220
  58.9 0.9 %copy-start.6 = (bf16[256,256]{1,0:T(8,128)(2,1)S(1)}, bf16[256,256]{1,0:T(8,128)(2,1)}, u32[]{:S(2)}) copy-start(bf16[256,256]{1,0:T(8,128)(2,1)} %param.21) | copy-start | bytes 393220
